TPU v7x, 32 devices: a whole 2x2x4 slice. The times are simulated.
32 devices in a mesh: ctx: 8 (over y, x, core), exp: 4 (over z).
Axes of the slice: x: 2, y: 2, z: 4, core: 2. Of those that a mesh axis runs over, the one named last changes fastest.
Arguments:
- queries: bfloat16 [512, 64, 512], P('ctx', 'exp'), may hold values from -17 to 17
- latent: bfloat16 [512, 512], P('ctx'), may hold values from -2 to 2
- grad_out: bfloat16 [512, 64, 512], P('ctx', 'exp'), may hold values from -6 to 6
- doc_ids: int32 [512], P('ctx'), may hold values from 0 to 5, as said below
- tokens: bfloat16 [4096, 7168], P(('ctx', 'exp')), may hold values from -6 to 6
- token_grads: bfloat16 [4096, 7168], P(('ctx', 'exp')), may hold values from -1.5 to 1.5
- gate_values: float32 [4096, 8], P(('ctx', 'exp')), may hold values from 0.3 to 3
- expert_ids: int32 [4096, 8], P(('ctx', 'exp')), may hold values from 0 to 255, as said below
- gate_order: int32 [32, 128], P(('ctx', 'exp')), may hold values from 0 to 127, each once within a row
- w_gate: bfloat16 [4, 7168, 2048], P('exp', None, 'ctx'), may hold values from -0.0625 to 0.0625
- w_up: bfloat16 [4, 7168, 2048], P('exp', None, 'ctx'), may hold values from -0.0625 to 0.0625
- w_down: bfloat16 [4, 2048, 7168], P('exp', 'ctx'), may hold values from -0.125 to 0.125
Outputs:
- d_queries: bfloat16 [512, 64, 512], P('ctx', 'exp')
- d_latent: bfloat16 [512, 512], P('ctx')
- d_tokens: bfloat16 [4096, 7168], P(('ctx', 'exp'))
- d_gates: bfloat16 [4096, 8], P(('ctx', 'exp'))
Inputs may be any that keep to these rules, and one draw needn't show every extreme that they name: `doc_ids`: never falling along the sequence; every number below 6 occurs. `expert_ids`: each row names 8 different experts. For every index of ctx some expert below 4 is named by 2 or more rows of every device at that index. `gate_order`: each row holds every number below 128 once.
All inputs are finite; a program needn't handle non-finite values.
Results may differ from a plain program's by a relative error of at most 0.02.
Values may be sent and summed in bfloat16 or wider, within the bound.
No kernel may reach another device: no remote copies, remote signals or barrier semaphores. Data moves between devices by JAX's collectives and lax.ppermute only.
A program may use at most 128 MiB of HBM per device.

v0:
```python
import jax
import jax.numpy as jnp
from jax import lax
from jax.sharding import PartitionSpec as P

SCALE_DIM = 192
CAP = 2


def passed_along(array, axis, by):
    count = lax.axis_size(axis)
    return lax.ppermute(array, axis, [(i, (i + by) % count) for i in range(count)])


def pass_keys(key_block):
    return passed_along(key_block, "ctx", 1)


def pass_grads(carried):
    return passed_along(carried.astype(jnp.bfloat16), "ctx", 1).astype(carried.dtype)


def attention_grads(queries, latent, grad_out, doc_ids):
    cycle_size = lax.axis_size("ctx")
    my_index = lax.axis_index("ctx")
    row_count = queries.shape[0]
    head_count = queries.shape[1]
    latent_width = queries.shape[2]
    softmax_scale = SCALE_DIM ** (-0.5)
    all_docs = lax.all_gather(doc_ids, "ctx", axis=0, tiled=True)

    def masked_scores(key_block, source):
        key_docs = lax.dynamic_slice_in_dim(all_docs, source * row_count, row_count)
        allowed = key_docs[None, :] == doc_ids[:, None]
        router_logits = softmax_scale * jnp.einsum(
            "qhl,kl->hqk", queries, key_block, preferred_element_type=jnp.float32
        )
        return jnp.where(allowed[None], router_logits, -1e30)

    def forward_visit(state, hop_index):
        key_block, prev_max, prev_sum, prev_out = state
        source = (my_index - hop_index) % cycle_size
        router_logits = masked_scores(key_block, source)
        new_max = jnp.maximum(prev_max, jnp.max(router_logits, axis=2))
        shrink = jnp.exp(prev_max - new_max)
        unnorm = jnp.exp(router_logits - new_max[:, :, None])
        new_sum = prev_sum * shrink + jnp.sum(unnorm, axis=2)
        new_out = prev_out * shrink[:, :, None] + jnp.einsum(
            "hqk,kl->hql",
            unnorm.astype(jnp.bfloat16),
            key_block,
            preferred_element_type=jnp.float32,
        )
        return (key_block, new_max, new_sum, new_out)

    def forward_hop(hop_index, state):
        state = forward_visit(state, hop_index)
        return (pass_keys(state[0]), state[1], state[2], state[3])

    start_state = (
        latent,
        jnp.full((head_count, row_count), -1e30, jnp.float32),
        jnp.zeros((head_count, row_count), jnp.float32),
        jnp.zeros((head_count, row_count, latent_width), jnp.float32),
    )
    state = lax.fori_loop(0, cycle_size - 1, forward_hop, start_state)
    state = forward_visit(state, cycle_size - 1)
    output = state[3] / state[2][:, :, None]
    log_sum = state[1] + jnp.log(state[2])
    delta_rows = jnp.einsum(
        "qhl,hql->hq", grad_out.astype(jnp.float32), output, precision=lax.Precision.HIGHEST
    )

    def backward_terms(key_block, source):
        router_logits = masked_scores(key_block, source)
        probs = jnp.exp(router_logits - log_sum[:, :, None])
        prob_grad = jnp.einsum(
            "qhl,kl->hqk", grad_out, key_block, preferred_element_type=jnp.float32
        )
        score_grad = (probs * (prob_grad - delta_rows[:, :, None])).astype(jnp.bfloat16)
        query_term = softmax_scale * jnp.einsum(
            "hqk,kl->qhl", score_grad, key_block, preferred_element_type=jnp.float32
        )
        latent_term = softmax_scale * jnp.einsum(
            "hqk,qhl->kl", score_grad, queries, preferred_element_type=jnp.float32
        )
        latent_term = latent_term + jnp.einsum(
            "hqk,qhl->kl", probs.astype(jnp.bfloat16), grad_out, preferred_element_type=jnp.float32
        )
        return (query_term, latent_term)

    query_start = jnp.zeros(queries.shape, jnp.float32)
    last_source = (my_index + 1) % cycle_size

    def carry_hop(hop_index, state):
        key_block, carried, query_acc = state
        source = (my_index - hop_index) % cycle_size
        query_term, latent_term = backward_terms(key_block, source)
        return (pass_keys(key_block), pass_grads(carried + latent_term), query_acc + query_term)

    state = lax.fori_loop(
        0, cycle_size - 1, carry_hop, (latent, jnp.zeros(latent.shape, jnp.float32), query_start)
    )
    query_term, latent_term = backward_terms(state[0], last_source)
    own_latent = pass_grads(state[1] + latent_term)
    query_acc = state[2] + query_term
    d_latent = lax.psum(own_latent.astype(jnp.bfloat16), "exp")
    return (query_acc.astype(jnp.bfloat16), d_latent)


def expert_grads(tokens, token_grads, gate_values, expert_ids, gate_order, w_gate, w_up, w_down):
    exp_size = lax.axis_size("exp")
    per_device = w_gate.shape[0]
    resident = per_device * exp_size
    model_width = tokens.shape[1]
    expert_span = jnp.arange(resident, dtype=jnp.int32)
    matches = (expert_ids[:, :, None] == expert_span).astype(jnp.int32)
    hits = jnp.sum(matches, axis=1)
    priority = gate_order[0]
    earlier = (priority[:, None] < priority[None, :]).astype(jnp.int32)
    ranks = jnp.einsum("ut,ue->te", earlier, hits)
    chosen = (hits[:, :, None] == 1) & (ranks[:, :, None] == jnp.arange(CAP, dtype=jnp.int32))
    picker = chosen.astype(jnp.bfloat16)
    send_in = jnp.einsum("tes,td->esd", picker, tokens, preferred_element_type=jnp.float32).astype(
        jnp.bfloat16
    )
    send_grad = jnp.einsum(
        "tes,td->esd", picker, token_grads, preferred_element_type=jnp.float32
    ).astype(jnp.bfloat16)
    recv_in, recv_grad = (
        lax.all_to_all(send_in, "exp", split_axis=0, concat_axis=0, tiled=True),
        lax.all_to_all(send_grad, "exp", split_axis=0, concat_axis=0, tiled=True),
    )
    recv_in = recv_in.reshape(exp_size, per_device, CAP, model_width)
    recv_grad = recv_grad.reshape(exp_size, per_device, CAP, model_width)
    piece_in = lax.all_gather(recv_in, "ctx", axis=0, tiled=True)
    piece_grad = lax.all_gather(recv_grad, "ctx", axis=0, tiled=True)
    gate_pre = jnp.einsum("necd,edh->nech", piece_in, w_gate, preferred_element_type=jnp.float32)
    up_pre = jnp.einsum("necd,edh->nech", piece_in, w_up, preferred_element_type=jnp.float32)
    act_grad = jnp.einsum("necd,ehd->nech", piece_grad, w_down, preferred_element_type=jnp.float32)
    gate_sig = jax.nn.sigmoid(gate_pre)
    silu_val = gate_pre * gate_sig
    hidden_act = (silu_val * up_pre).astype(jnp.bfloat16)
    score_part = jnp.sum(hidden_act.astype(jnp.float32) * act_grad, axis=3)
    gate_grad = (act_grad * up_pre * gate_sig * (1.0 + gate_pre * (1.0 - gate_sig))).astype(
        jnp.bfloat16
    )
    up_grad = (act_grad * silu_val).astype(jnp.bfloat16)
    term = jnp.einsum("nech,edh->necd", gate_grad, w_gate, preferred_element_type=jnp.float32)
    row_sums = lax.psum_scatter(
        (
            term + jnp.einsum("nech,edh->necd", up_grad, w_up, preferred_element_type=jnp.float32)
        ).astype(jnp.bfloat16),
        "ctx",
        scatter_dimension=0,
        tiled=True,
    )
    score_sums = lax.psum_scatter(score_part, "ctx", scatter_dimension=0, tiled=True)
    back_rows, back_scores = (
        lax.all_to_all(row_sums, "exp", split_axis=0, concat_axis=0, tiled=True),
        lax.all_to_all(
            score_sums.astype(jnp.bfloat16), "exp", split_axis=0, concat_axis=0, tiled=True
        ),
    )
    back_rows = back_rows.reshape(resident, CAP, model_width)
    back_scores = back_scores.reshape(resident, CAP)
    gate_mass = jnp.sum(matches.astype(jnp.float32) * gate_values[:, :, None], axis=1)
    weighting = chosen.astype(jnp.float32) * gate_mass[:, :, None]
    d_tokens = jnp.einsum(
        "tes,esd->td", weighting, back_rows.astype(jnp.float32), precision=lax.Precision.HIGHEST
    )
    kept_scores = jnp.einsum(
        "tes,es->te",
        chosen.astype(jnp.float32),
        back_scores.astype(jnp.float32),
        precision=lax.Precision.HIGHEST,
    )
    d_gates = jnp.einsum(
        "tke,te->tk", matches.astype(jnp.float32), kept_scores, precision=lax.Precision.HIGHEST
    )
    return (d_tokens.astype(jnp.bfloat16), d_gates.astype(jnp.bfloat16))


def local(
    queries,
    latent,
    grad_out,
    doc_ids,
    tokens,
    token_grads,
    gate_values,
    expert_ids,
    gate_order,
    w_gate,
    w_up,
    w_down,
):
    d_queries, d_latent = attention_grads(queries, latent, grad_out, doc_ids)
    d_tokens, d_gates = expert_grads(
        tokens, token_grads, gate_values, expert_ids, gate_order, w_gate, w_up, w_down
    )
    return (d_queries, d_latent, d_tokens, d_gates)


def solution(mesh):
    in_specs = (
        P("ctx", "exp", None),
        P("ctx", None),
        P("ctx", "exp", None),
        P("ctx"),
        P(("ctx", "exp"), None),
        P(("ctx", "exp"), None),
        P(("ctx", "exp"), None),
        P(("ctx", "exp"), None),
        P(("ctx", "exp"), None),
        P("exp", None, "ctx"),
        P("exp", None, "ctx"),
        P("exp", "ctx", None),
    )
    out_specs = (
        P("ctx", "exp", None),
        P("ctx", None),
        P(("ctx", "exp"), None),
        P(("ctx", "exp"), None),
    )
    return jax.shard_map(local, mesh=mesh, in_specs=in_specs, out_specs=out_specs, check_vma=False)
```

profile of v0, /device:TPU:0, one launch (start us, length us, event | category | flops | bytes accessed | tf_op | source)
XLA Modules:
  0.0 247.9 jit_solution(17384847041630404391)
XLA Ops:
  7.2 1.0 copy.157
  8.2 1.3 fusion.108
  10.2 0.9 dynamic-update-slice
  11.0 9.5 %all-reduce = s32[512]{0:T(512)S(1)} all-reduce(s32[512]{0:T(512)S(1)} %dynamic-update-slice), channel_id=1, replica_groups=mesh['ctx'=8,'exp'=4] {'ctx'}, use_global_device_ids=true, to_apply=%add | all-reduce | flops 512 | bytes 4096
  20.5 1.9 copy.57
  22.4 1.5 copy.58
  24.2 32.2 %while.42 = (s32[]{:T(128)}, bf16[64,512]{1,0:T(8,128)(2,1)S(1)}, f32[16,64]{1,0:T(8,128)S(1)}, f32[16,64]{1,0:T(8,128)S(1)}, f32[16,64,512]{2,1,0:T(8,128)}, /*...) while((s32[]{:T(128)}, bf16[64,512]{1,0:T(8,128)(2,1)S(1)}, ...), condition=%wide.region_3.4_spmd.clone, body=%wide.region_0.3_spmd.clone.sunk | while | flops 136258576 | bytes 23405988 | solution.py:66
  26.4 1.3 copy-done.3
  27.7 1.1 collective-permute-done
  31.0 1.3 copy-done.3
  32.3 1.1 collective-permute-done
  35.6 1.3 copy-done.3
  36.9 1.1 collective-permute-done
  40.2 1.3 copy-done.3
  41.5 1.1 collective-permute-done
  44.8 1.3 copy-done.3
  46.1 1.1 collective-permute-done
  49.4 1.3 copy-done.3
  50.7 1.1 collective-permute-done
  54.0 1.3 copy-done.3
  55.3 1.1 collective-permute-done
  56.4 2.7 %fusion.109 = (f32[16,64]{1,0:T(8,128)S(1)}, f32[16,64,64]{1,2,0:T(8,128)S(1)}) fusion(bf16[64,16,512]{2,1,0:T(8,128)(2,1)} %param.16, bf16[64,512]{1,0:T(8,128)(2,1)S(1)} %get-tuple-element.496, pred[64,64]{0,1:T(8,128)(4,1)S(1)} %get-tuple-element.692), kind=kOutput, calls=%fused_computation.142 | convolution fusion | flops 67304448 | bytes 1384448 | tf_op jit(solution)/shard_map/qhl,kl->hqk/dot_general | solution.py:35
  60.5 1.2 multiply_reduce_fusion
  61.8 51.8 %while.43 = (s32[]{:T(128)}, bf16[64,512]{1,0:T(8,128)(2,1)S(1)}, f32[64,512]{1,0:T(8,128)S(1)}, f32[64,16,512]{2,0,1:T(8,128)}, s32[]{:T(128)}, /*index=5*/s32[...) while((s32[]{:T(128)}, bf16[64,512]{1,0:T(8,128)(2,1)S(1)}, ...), condition=%wide.region_7.8_spmd.clone, body=%wide.region_6.7_spmd.clone.sunk | while | flops 337776640 | bytes 15287743 | solution.py:101
  64.5 1.8 bitcast_add_fusion.3
  66.3 2.8 %collective-permute-done.2 = bf16[64,512]{1,0:T(8,128)(2,1)S(1)} collective-permute-done((bf16[64,512]{1,0:T(8,128)(2,1)S(1)}, bf16[64,512]{1,0:T(8,128)(2,1)S(1)}, u32[]{:S(2)}, u32[]{:S(2)}) %collective-permute-start.2) | collective-permute-done | bytes 65568 | tf_op jit(solution)/shard_map/while/body/eval_jaxpr/ppermute | solution.py:12
  71.9 3.4 %bitcast_add_fusion.3 = f32[64,16,512]{2,0,1:T(8,128)} fusion(f32[64,16,512]{2,0,1:T(8,128)} %get-tuple-element.892, bf16[16,64,64]{1,2,0:T(8,128)(2,1)S(1)} %fusion.160, pred[]{:T(512)S(6)} %compare.11, bf16[64,512]{1,0:T(8,128)(2,1)S(1)} %copy.146), kind=kOutput, calls=%fused_computation.16.clone.1 | convolution fusion | flops 68681728 | bytes 4390913 | tf_op jit(solution)/shard_map/while/body/eval_jaxpr/hqk,kl->qhl/dot_general | solution.py:81
  75.3 1.1 collective-permute-done.2
  79.1 1.0 collective-permute-start.2
  80.1 3.4 %bitcast_add_fusion.3 = f32[64,16,512]{2,0,1:T(8,128)} fusion(f32[64,16,512]{2,0,1:T(8,128)} %get-tuple-element.892, bf16[16,64,64]{1,2,0:T(8,128)(2,1)S(1)} %fusion.160, pred[]{:T(512)S(6)} %compare.11, bf16[64,512]{1,0:T(8,128)(2,1)S(1)} %copy.146), kind=kOutput, calls=%fused_computation.16.clone.1 | convolution fusion | flops 68681728 | bytes 4390913 | tf_op jit(solution)/shard_map/while/body/eval_jaxpr/hqk,kl->qhl/dot_general | solution.py:81
  86.4 1.0 collective-permute-start.2
  87.4 3.4 %bitcast_add_fusion.3 = f32[64,16,512]{2,0,1:T(8,128)} fusion(f32[64,16,512]{2,0,1:T(8,128)} %get-tuple-element.892, bf16[16,64,64]{1,2,0:T(8,128)(2,1)S(1)} %fusion.160, pred[]{:T(512)S(6)} %compare.11, bf16[64,512]{1,0:T(8,128)(2,1)S(1)} %copy.146), kind=kOutput, calls=%fused_computation.16.clone.1 | convolution fusion | flops 68681728 | bytes 4390913 | tf_op jit(solution)/shard_map/while/body/eval_jaxpr/hqk,kl->qhl/dot_general | solution.py:81
  93.8 1.7 collective-permute-start.2
  95.5 3.4 %bitcast_add_fusion.3 = f32[64,16,512]{2,0,1:T(8,128)} fusion(f32[64,16,512]{2,0,1:T(8,128)} %get-tuple-element.892, bf16[16,64,64]{1,2,0:T(8,128)(2,1)S(1)} %fusion.160, pred[]{:T(512)S(6)} %compare.11, bf16[64,512]{1,0:T(8,128)(2,1)S(1)} %copy.146), kind=kOutput, calls=%fused_computation.16.clone.1 | convolution fusion | flops 68681728 | bytes 4390913 | tf_op jit(solution)/shard_map/while/body/eval_jaxpr/hqk,kl->qhl/dot_general | solution.py:81
  101.6 1.2 collective-permute-start.2
  102.8 3.4 %bitcast_add_fusion.3 = f32[64,16,512]{2,0,1:T(8,128)} fusion(f32[64,16,512]{2,0,1:T(8,128)} %get-tuple-element.892, bf16[16,64,64]{1,2,0:T(8,128)(2,1)S(1)} %fusion.160, pred[]{:T(512)S(6)} %compare.11, bf16[64,512]{1,0:T(8,128)(2,1)S(1)} %copy.146), kind=kOutput, calls=%fused_computation.16.clone.1 | convolution fusion | flops 68681728 | bytes 4390913 | tf_op jit(solution)/shard_map/while/body/eval_jaxpr/hqk,kl->qhl/dot_general | solution.py:81
  108.9 1.2 collective-permute-start.2
  110.1 3.4 %bitcast_add_fusion.3 = f32[64,16,512]{2,0,1:T(8,128)} fusion(f32[64,16,512]{2,0,1:T(8,128)} %get-tuple-element.892, bf16[16,64,64]{1,2,0:T(8,128)(2,1)S(1)} %fusion.160, pred[]{:T(512)S(6)} %compare.11, bf16[64,512]{1,0:T(8,128)(2,1)S(1)} %copy.146), kind=kOutput, calls=%fused_computation.16.clone.1 | convolution fusion | flops 68681728 | bytes 4390913 | tf_op jit(solution)/shard_map/while/body/eval_jaxpr/hqk,kl->qhl/dot_general | solution.py:81
  113.6 2.7 %fusion.45 = f32[16,64,64]{1,2,0:T(8,128)S(1)} fusion(f32[16,64]{1,0:T(8,128)S(1)} %get-tuple-element.946, pred[64,64]{0,1:T(8,128)(4,1)S(1)} %get-tuple-element.691, bf16[64,512]{1,0:T(8,128)(2,1)S(1)} %get-tuple-element.500, bf16[64,16,512]{2,1,0:T(8,128)(2,1)} %param.16), kind=kOutput, calls=%fused_computation.66 | convolution fusion | flops 67305472 | bytes 1384448 | tf_op jit(solution)/shard_map/qhl,kl->hqk/dot_general | solution.py:35
  116.3 1.3 fusion.48
  117.7 1.2 convolution_bitcast_fusion.5
  118.9 1.2 fusion.52
  120.9 0.7 copy.66
  121.6 4.9 %all-to-all-start.1 = ((bf16[4,2,7168]{2,1,0:T(2,128)(2,1)}), bf16[4,2,7168]{2,1,0:T(2,128)(2,1)S(1)}, u32[]{:S(2)}, u32[]{:S(2)}) async-start(bf16[4,2,7168]{2,1,0:T(2,128)(2,1)} %copy.66), calls=%async_computation.1 | async-start | bytes 229376 | tf_op jit(solution)/shard_map/all_to_all | solution.py:131
  126.5 2.5 %convolution_convert_fusion.1 = bf16[4,2,7168]{2,1,0:T(2,128)(2,1)} fusion(bf16[128,7168]{1,0:T(8,128)(2,1)} %param.21, pred[128,4,2]{0,1,2:T(4,128)(4,1)S(1)} %fusion.95), kind=kOutput, calls=%fused_computation.43 | convolution fusion | flops 14737408 | bytes 1950720 | tf_op jit(solution)/shard_map/tes,td->esd/dot_general | solution.py:127
  129.7 3.3 %all-to-all-done.1 = bf16[4,2,7168]{2,1,0:T(2,128)(2,1)S(1)} async-done(((bf16[4,2,7168]{2,1,0:T(2,128)(2,1)}), bf16[4,2,7168]{2,1,0:T(2,128)(2,1)S(1)}, u32[]{:S(2)}, u32[]{:S(2)}) %all-to-all-start.1) | async-done | bytes 114720 | tf_op jit(solution)/shard_map/all_to_all | solution.py:131
  133.0 3.5 %all-to-all-start = ((bf16[4,2,7168]{2,1,0:T(2,128)(2,1)}), bf16[4,2,7168]{2,1,0:T(2,128)(2,1)S(1)}, u32[]{:S(2)}, u32[]{:S(2)}) async-start(bf16[4,2,7168]{2,1,0:T(2,128)(2,1)} %convolution_convert_fusion.1), calls=%async_computation | async-start | bytes 229376 | tf_op jit(solution)/shard_map/all_to_all | solution.py:132
  136.5 10.4 %all-gather.1 = bf16[32,2,7168]{2,1,0:T(2,128)(2,1)S(1)} all-gather(bf16[4,2,7168]{2,1,0:T(2,128)(2,1)S(1)} %all-to-all-done.1), channel_id=3, replica_groups=mesh['ctx'=8,'exp'=4] {'ctx'}, dimensions={0}, use_global_device_ids=true | all-gather | bytes 1032192 | tf_op jit(solution)/shard_map/all_gather | solution.py:136
  146.9 2.8 %fusion.59 = f32[32,1,2,256]{3,0,2,1:T(8,128)S(1)} fusion(bf16[1,7168,256]{2,1,0:T(8,128)(2,1)} %param.25, bf16[32,2,7168]{2,1,0:T(2,128)(2,1)S(1)} %all-gather.1), kind=kOutput, calls=%fused_computation.79 | convolution fusion | flops 234881024 | bytes 4653056 | tf_op jit(solution)/shard_map/necd,edh->nech/dot_general | solution.py:138
  150.8 10.3 %all-gather = bf16[32,2,7168]{2,1,0:T(2,128)(2,1)S(1)} all-gather(bf16[4,2,7168]{2,1,0:T(2,128)(2,1)S(1)} %all-to-all-done), channel_id=2, replica_groups=mesh['ctx'=8,'exp'=4] {'ctx'}, dimensions={0}, use_global_device_ids=true | all-gather | bytes 1032192 | tf_op jit(solution)/shard_map/all_gather | solution.py:137
  161.0 3.5 %multiply_reduce_fusion.1 = (f32[32,2]{0,1:T(2,128)S(1)}, f32[32,1,2,256]{3,0,2,1:T(8,128)S(1)}) fusion(f32[32,1,2,256]{3,0,2,1:T(8,128)S(1)} %fusion.56, f32[32,1,2,256]{3,0,2,1:T(8,128)S(1)} %fusion.59, bf16[1,256,7168]{2,1,0:T(8,128)(2,1)} %param.27, bf16[32,2,7168]{2,1,0:T(2,128)(2,1)S(1)} %all-gather), kind=kOutput, calls=%fused_computation.95 | convolution fusion | flops 235028416 | bytes 4784384 | tf_op jit(solution)/shard_map/necd,ehd->nech/dot_general | solution.py:140
  164.6 1.2 fusion.28
  165.8 0.8 copy-done.6
  166.6 2.1 fusion.27
  168.8 2.1 fusion.37
  170.9 1.5 copy.73
  173.1 13.4 %all-reduce.2 = bf16[32,1,2]{0,2,1:T(2,128)(2,1)S(1)} all-reduce(f32[32,1,2]{0,2,1:T(2,128)S(1)} %bitcast.233), channel_id=5, replica_groups=mesh['ctx'=8,'exp'=4] {'ctx'}, use_global_device_ids=true, to_apply=%region_13.14.clone | all-reduce | flops 64 | bytes 384
  186.7 10.2 %all_to_all.20 = bf16[4,1,2]{2,1,0:T(2,128)(2,1)S(1)} all-to-all(bf16[4,1,2]{2,1,0:T(2,128)(2,1)S(1)} %copy.71), channel_id=1, replica_groups=mesh['ctx'=8,'exp'=4] {'exp'}, dimensions={0} | all-to-all | bytes 32 | tf_op jit(solution)/shard_map/all_to_all | solution.py:161
  197.1 28.2 %all-reduce.8.cloned.1.call-done = bf16[32,1,2,7168]{3,0,2,1:T(8,128)(2,1)} async-done(((bf16[32,1,2,7168]{3,0,2,1:T(8,128)(2,1)}), bf16[32,1,2,7168]{3,0,2,1:T(8,128)(2,1)}) %all-reduce.8.cloned.1.call-update) | async-done | bytes 917520
  225.3 1.0 constant_dynamic-slice_fusion
  226.4 0.7 copy.69
  227.1 4.5 %all-to-all-start.2 = ((bf16[4,1,2,7168]{3,2,1,0:T(2,128)(2,1)}), bf16[4,1,2,7168]{3,2,1,0:T(2,128)(2,1)S(1)}, u32[]{:S(2)}, u32[]{:S(2)}) async-start(bf16[4,1,2,7168]{3,2,1,0:T(2,128)(2,1)} %copy.69), calls=%async_computation.2 | async-start | bytes 229376 | tf_op jit(solution)/shard_map/all_to_all | solution.py:160
  232.3 5.2 %all-to-all-done.2 = bf16[4,1,2,7168]{3,2,1,0:T(2,128)(2,1)S(1)} async-done(((bf16[4,1,2,7168]{3,2,1,0:T(2,128)(2,1)}), bf16[4,1,2,7168]{3,2,1,0:T(2,128)(2,1)S(1)}, u32[]{:S(2)}, u32[]{:S(2)}) %all-to-all-start.2) | async-done | bytes 114720 | tf_op jit(solution)/shard_map/all_to_all | solution.py:160
  237.5 2.9 %fusion.25 = bf16[128,7168]{1,0:T(8,128)(2,1)} fusion(bf16[4,1,2,7168]{3,2,1,0:T(2,128)(2,1)S(1)} %all-to-all-done.2, pred[128,4,2]{0,1,2:T(4,128)(4,1)S(1)} %fusion.95, f32[128,4]{0,1:T(4,128)S(1)} %fusion.87), kind=kOutput, calls=%fused_computation.38 | convolution fusion | flops 88998912 | bytes 1952768 | tf_op jit(solution)/shard_map/tes,esd->td/dot_general | solution.py:169
  (247 shorter events, 39.6 us)
Async XLA Ops:
  7.2 113.4 %copy-start = (bf16[128,7168]{1,0:T(8,128)(2,1)S(1)}, bf16[128,7168]{1,0:T(8,128)(2,1)}, u32[]{:S(2)}) copy-start(bf16[128,7168]{1,0:T(8,128)(2,1)} %param.20) | copy-start | bytes 5505028
  20.5 1.9 copy-start.8
  20.5 3.5 %copy-start.14 = (s32[64]{0:T(128)S(1)}, s32[64]{0:T(128)}, u32[]{:S(2)}) copy-start(s32[64]{0:T(128)} %param.19) | copy-start | bytes 772
  24.2 4.6 %collective-permute-start = (bf16[64,512]{1,0:T(8,128)(2,1)S(1)}, bf16[64,512]{1,0:T(8,128)(2,1)S(1)}, u32[]{:S(2)}, u32[]{:S(2)}) collective-permute-start(bf16[64,512]{1,0:T(8,128)(2,1)S(1)} %copy.132), channel_id=1, source_target_pairs={{0,4},{4,8},{8,12},{12,16},{16,20},{20,24},{24,28},{28,0},{1,5},{5... | collective-permute-start | bytes 196616 | tf_op jit(solution)/shard_map/while/body/eval_jaxpr/ppermute | solution.py:12
  24.3 1.6 copy-start.2
  26.4 1.3 copy-start.3
  28.8 4.6 %collective-permute-start = (bf16[64,512]{1,0:T(8,128)(2,1)S(1)}, bf16[64,512]{1,0:T(8,128)(2,1)S(1)}, u32[]{:S(2)}, u32[]{:S(2)}) collective-permute-start(bf16[64,512]{1,0:T(8,128)(2,1)S(1)} %copy.132), channel_id=1, source_target_pairs={{0,4},{4,8},{8,12},{12,16},{16,20},{20,24},{24,28},{28,0},{1,5},{5... | collective-permute-start | bytes 196616 | tf_op jit(solution)/shard_map/while/body/eval_jaxpr/ppermute | solution.py:12
  28.9 1.6 copy-start.2
  31.0 1.3 copy-start.3
  33.4 4.6 %collective-permute-start = (bf16[64,512]{1,0:T(8,128)(2,1)S(1)}, bf16[64,512]{1,0:T(8,128)(2,1)S(1)}, u32[]{:S(2)}, u32[]{:S(2)}) collective-permute-start(bf16[64,512]{1,0:T(8,128)(2,1)S(1)} %copy.132), channel_id=1, source_target_pairs={{0,4},{4,8},{8,12},{12,16},{16,20},{20,24},{24,28},{28,0},{1,5},{5... | collective-permute-start | bytes 196616 | tf_op jit(solution)/shard_map/while/body/eval_jaxpr/ppermute | solution.py:12
  33.5 1.6 copy-start.2
  35.6 1.3 copy-start.3
  38.0 4.6 %collective-permute-start = (bf16[64,512]{1,0:T(8,128)(2,1)S(1)}, bf16[64,512]{1,0:T(8,128)(2,1)S(1)}, u32[]{:S(2)}, u32[]{:S(2)}) collective-permute-start(bf16[64,512]{1,0:T(8,128)(2,1)S(1)} %copy.132), channel_id=1, source_target_pairs={{0,4},{4,8},{8,12},{12,16},{16,20},{20,24},{24,28},{28,0},{1,5},{5... | collective-permute-start | bytes 196616 | tf_op jit(solution)/shard_map/while/body/eval_jaxpr/ppermute | solution.py:12
  38.1 1.6 copy-start.2
  40.2 1.3 copy-start.3
  42.6 4.6 %collective-permute-start = (bf16[64,512]{1,0:T(8,128)(2,1)S(1)}, bf16[64,512]{1,0:T(8,128)(2,1)S(1)}, u32[]{:S(2)}, u32[]{:S(2)}) collective-permute-start(bf16[64,512]{1,0:T(8,128)(2,1)S(1)} %copy.132), channel_id=1, source_target_pairs={{0,4},{4,8},{8,12},{12,16},{16,20},{20,24},{24,28},{28,0},{1,5},{5... | collective-permute-start | bytes 196616 | tf_op jit(solution)/shard_map/while/body/eval_jaxpr/ppermute | solution.py:12
  42.7 1.6 copy-start.2
  44.8 1.3 copy-start.3
  47.2 4.6 %collective-permute-start = (bf16[64,512]{1,0:T(8,128)(2,1)S(1)}, bf16[64,512]{1,0:T(8,128)(2,1)S(1)}, u32[]{:S(2)}, u32[]{:S(2)}) collective-permute-start(bf16[64,512]{1,0:T(8,128)(2,1)S(1)} %copy.132), channel_id=1, source_target_pairs={{0,4},{4,8},{8,12},{12,16},{16,20},{20,24},{24,28},{28,0},{1,5},{5... | collective-permute-start | bytes 196616 | tf_op jit(solution)/shard_map/while/body/eval_jaxpr/ppermute | solution.py:12
  47.3 1.6 copy-start.2
  49.4 1.3 copy-start.3
  51.8 4.6 %collective-permute-start = (bf16[64,512]{1,0:T(8,128)(2,1)S(1)}, bf16[64,512]{1,0:T(8,128)(2,1)S(1)}, u32[]{:S(2)}, u32[]{:S(2)}) collective-permute-start(bf16[64,512]{1,0:T(8,128)(2,1)S(1)} %copy.132), channel_id=1, source_target_pairs={{0,4},{4,8},{8,12},{12,16},{16,20},{20,24},{24,28},{28,0},{1,5},{5... | collective-permute-start | bytes 196616 | tf_op jit(solution)/shard_map/while/body/eval_jaxpr/ppermute | solution.py:12
  51.8 1.6 copy-start.2
  54.0 1.3 copy-start.3
  56.4 2.9 %copy-start.4 = (f32[16,64,512]{2,1,0:T(8,128)S(1)}, f32[16,64,512]{2,1,0:T(8,128)}, u32[]{:S(2)}) copy-start(f32[16,64,512]{2,1,0:T(8,128)} %get-tuple-element.498) | copy-start | bytes 6291460
  59.3 1.2 copy-start.9
  61.8 7.3 %collective-permute-start.1 = (bf16[64,512]{1,0:T(8,128)(2,1)S(1)}, bf16[64,512]{1,0:T(8,128)(2,1)S(1)}, u32[]{:S(2)}, u32[]{:S(2)}) collective-permute-start(bf16[64,512]{1,0:T(8,128)(2,1)S(1)} %copy.146), channel_id=1, source_target_pairs={{0,4},{4,8},{8,12},{12,16},{16,20},{20,24},{24,28},{28,0},{1,5},{5... | collective-permute-start | bytes 196616 | tf_op jit(solution)/shard_map/while/body/eval_jaxpr/ppermute | solution.py:12
  61.9 1.2 copy-start.1
  64.5 4.6 %collective-permute-start.2 = (bf16[64,512]{1,0:T(8,128)(2,1)S(1)}, bf16[64,512]{1,0:T(8,128)(2,1)S(1)}, u32[]{:S(2)}, u32[]{:S(2)}) collective-permute-start(bf16[64,512]{1,0:T(8,128)(2,1)S(1)} %fusion.161), channel_id=1, source_target_pairs={{0,4},{4,8},{8,12},{12,16},{16,20},{20,24},{24,28},{28,0},{1,5},{5... | collective-permute-start | bytes 196616 | tf_op jit(solution)/shard_map/while/body/eval_jaxpr/ppermute | solution.py:12
  69.1 7.3 %collective-permute-start.1 = (bf16[64,512]{1,0:T(8,128)(2,1)S(1)}, bf16[64,512]{1,0:T(8,128)(2,1)S(1)}, u32[]{:S(2)}, u32[]{:S(2)}) collective-permute-start(bf16[64,512]{1,0:T(8,128)(2,1)S(1)} %copy.146), channel_id=1, source_target_pairs={{0,4},{4,8},{8,12},{12,16},{16,20},{20,24},{24,28},{28,0},{1,5},{5... | collective-permute-start | bytes 196616 | tf_op jit(solution)/shard_map/while/body/eval_jaxpr/ppermute | solution.py:12
  69.2 1.2 copy-start.1
  71.8 4.6 %collective-permute-start.2 = (bf16[64,512]{1,0:T(8,128)(2,1)S(1)}, bf16[64,512]{1,0:T(8,128)(2,1)S(1)}, u32[]{:S(2)}, u32[]{:S(2)}) collective-permute-start(bf16[64,512]{1,0:T(8,128)(2,1)S(1)} %fusion.161), channel_id=1, source_target_pairs={{0,4},{4,8},{8,12},{12,16},{16,20},{20,24},{24,28},{28,0},{1,5},{5... | collective-permute-start | bytes 196616 | tf_op jit(solution)/shard_map/while/body/eval_jaxpr/ppermute | solution.py:12
  76.5 7.3 %collective-permute-start.1 = (bf16[64,512]{1,0:T(8,128)(2,1)S(1)}, bf16[64,512]{1,0:T(8,128)(2,1)S(1)}, u32[]{:S(2)}, u32[]{:S(2)}) collective-permute-start(bf16[64,512]{1,0:T(8,128)(2,1)S(1)} %copy.146), channel_id=1, source_target_pairs={{0,4},{4,8},{8,12},{12,16},{16,20},{20,24},{24,28},{28,0},{1,5},{5... | collective-permute-start | bytes 196616 | tf_op jit(solution)/shard_map/while/body/eval_jaxpr/ppermute | solution.py:12
  76.6 1.2 copy-start.1
  79.1 4.6 %collective-permute-start.2 = (bf16[64,512]{1,0:T(8,128)(2,1)S(1)}, bf16[64,512]{1,0:T(8,128)(2,1)S(1)}, u32[]{:S(2)}, u32[]{:S(2)}) collective-permute-start(bf16[64,512]{1,0:T(8,128)(2,1)S(1)} %fusion.161), channel_id=1, source_target_pairs={{0,4},{4,8},{8,12},{12,16},{16,20},{20,24},{24,28},{28,0},{1,5},{5... | collective-permute-start | bytes 196616 | tf_op jit(solution)/shard_map/while/body/eval_jaxpr/ppermute | solution.py:12
  83.8 7.3 %collective-permute-start.1 = (bf16[64,512]{1,0:T(8,128)(2,1)S(1)}, bf16[64,512]{1,0:T(8,128)(2,1)S(1)}, u32[]{:S(2)}, u32[]{:S(2)}) collective-permute-start(bf16[64,512]{1,0:T(8,128)(2,1)S(1)} %copy.146), channel_id=1, source_target_pairs={{0,4},{4,8},{8,12},{12,16},{16,20},{20,24},{24,28},{28,0},{1,5},{5... | collective-permute-start | bytes 196616 | tf_op jit(solution)/shard_map/while/body/eval_jaxpr/ppermute | solution.py:12
  83.9 1.2 copy-start.1
  86.4 4.6 %collective-permute-start.2 = (bf16[64,512]{1,0:T(8,128)(2,1)S(1)}, bf16[64,512]{1,0:T(8,128)(2,1)S(1)}, u32[]{:S(2)}, u32[]{:S(2)}) collective-permute-start(bf16[64,512]{1,0:T(8,128)(2,1)S(1)} %fusion.161), channel_id=1, source_target_pairs={{0,4},{4,8},{8,12},{12,16},{16,20},{20,24},{24,28},{28,0},{1,5},{5... | collective-permute-start | bytes 196616 | tf_op jit(solution)/shard_map/while/body/eval_jaxpr/ppermute | solution.py:12
  91.1 7.8 %collective-permute-start.1 = (bf16[64,512]{1,0:T(8,128)(2,1)S(1)}, bf16[64,512]{1,0:T(8,128)(2,1)S(1)}, u32[]{:S(2)}, u32[]{:S(2)}) collective-permute-start(bf16[64,512]{1,0:T(8,128)(2,1)S(1)} %copy.146), channel_id=1, source_target_pairs={{0,4},{4,8},{8,12},{12,16},{16,20},{20,24},{24,28},{28,0},{1,5},{5... | collective-permute-start | bytes 196616 | tf_op jit(solution)/shard_map/while/body/eval_jaxpr/ppermute | solution.py:12
  91.2 1.2 copy-start.1
  93.8 5.1 %collective-permute-start.2 = (bf16[64,512]{1,0:T(8,128)(2,1)S(1)}, bf16[64,512]{1,0:T(8,128)(2,1)S(1)}, u32[]{:S(2)}, u32[]{:S(2)}) collective-permute-start(bf16[64,512]{1,0:T(8,128)(2,1)S(1)} %fusion.161), channel_id=1, source_target_pairs={{0,4},{4,8},{8,12},{12,16},{16,20},{20,24},{24,28},{28,0},{1,5},{5... | collective-permute-start | bytes 196616 | tf_op jit(solution)/shard_map/while/body/eval_jaxpr/ppermute | solution.py:12
  98.9 7.3 %collective-permute-start.1 = (bf16[64,512]{1,0:T(8,128)(2,1)S(1)}, bf16[64,512]{1,0:T(8,128)(2,1)S(1)}, u32[]{:S(2)}, u32[]{:S(2)}) collective-permute-start(bf16[64,512]{1,0:T(8,128)(2,1)S(1)} %copy.146), channel_id=1, source_target_pairs={{0,4},{4,8},{8,12},{12,16},{16,20},{20,24},{24,28},{28,0},{1,5},{5... | collective-permute-start | bytes 196616 | tf_op jit(solution)/shard_map/while/body/eval_jaxpr/ppermute | solution.py:12
  99.0 1.2 copy-start.1
  101.6 4.6 %collective-permute-start.2 = (bf16[64,512]{1,0:T(8,128)(2,1)S(1)}, bf16[64,512]{1,0:T(8,128)(2,1)S(1)}, u32[]{:S(2)}, u32[]{:S(2)}) collective-permute-start(bf16[64,512]{1,0:T(8,128)(2,1)S(1)} %fusion.161), channel_id=1, source_target_pairs={{0,4},{4,8},{8,12},{12,16},{16,20},{20,24},{24,28},{28,0},{1,5},{5... | collective-permute-start | bytes 196616 | tf_op jit(solution)/shard_map/while/body/eval_jaxpr/ppermute | solution.py:12
  106.3 7.3 %collective-permute-start.1 = (bf16[64,512]{1,0:T(8,128)(2,1)S(1)}, bf16[64,512]{1,0:T(8,128)(2,1)S(1)}, u32[]{:S(2)}, u32[]{:S(2)}) collective-permute-start(bf16[64,512]{1,0:T(8,128)(2,1)S(1)} %copy.146), channel_id=1, source_target_pairs={{0,4},{4,8},{8,12},{12,16},{16,20},{20,24},{24,28},{28,0},{1,5},{5... | collective-permute-start | bytes 196616 | tf_op jit(solution)/shard_map/while/body/eval_jaxpr/ppermute | solution.py:12
  106.4 1.2 copy-start.1
  108.9 4.6 %collective-permute-start.2 = (bf16[64,512]{1,0:T(8,128)(2,1)S(1)}, bf16[64,512]{1,0:T(8,128)(2,1)S(1)}, u32[]{:S(2)}, u32[]{:S(2)}) collective-permute-start(bf16[64,512]{1,0:T(8,128)(2,1)S(1)} %fusion.161), channel_id=1, source_target_pairs={{0,4},{4,8},{8,12},{12,16},{16,20},{20,24},{24,28},{28,0},{1,5},{5... | collective-permute-start | bytes 196616 | tf_op jit(solution)/shard_map/while/body/eval_jaxpr/ppermute | solution.py:12
  113.6 2.7 %copy-start.10 = (bf16[64,16,512]{2,1,0:T(8,128)(2,1)S(1)}, bf16[64,16,512]{2,1,0:T(8,128)(2,1)}, u32[]{:S(2)}) copy-start(bf16[64,16,512]{2,1,0:T(8,128)(2,1)} %param.18) | copy-start | bytes 3145732
  116.3 2.6 %copy-start.11 = (bf16[64,16,512]{2,1,0:T(8,128)(2,1)S(1)}, bf16[64,16,512]{2,1,0:T(8,128)(2,1)}, u32[]{:S(2)}) copy-start(bf16[64,16,512]{2,1,0:T(8,128)(2,1)} %param.16) | copy-start | bytes 3145732
  117.6 2.6 %copy-start.15 = (s32[128,8]{0,1:T(8,128)S(1)}, s32[128,8]{0,1:T(8,128)}, u32[]{:S(2)}) copy-start(s32[128,8]{0,1:T(8,128)} %param.23) | copy-start | bytes 12292
  117.7 2.7 %copy-start.17 = (s32[1,128]{1,0:T(1,128)S(1)}, s32[1,128]{1,0:T(1,128)}, u32[]{:S(2)}) copy-start(s32[1,128]{1,0:T(1,128)} %param.24) | copy-start | bytes 1540
  120.2 8.8 %collective-permute-start.3 = (bf16[64,512]{1,0:T(8,128)(2,1)S(1)}, bf16[64,512]{1,0:T(8,128)(2,1)S(1)}, u32[]{:S(2)}, u32[]{:S(2)}) collective-permute-start(bf16[64,512]{1,0:T(8,128)(2,1)S(1)} %fusion.52), channel_id=1, source_target_pairs={{0,4},{4,8},{8,12},{12,16},{16,20},{20,24},{24,28},{28,0},{1,5},{5... | collective-permute-start | bytes 196616 | tf_op jit(solution)/shard_map/ppermute | solution.py:12
  121.6 11.3 %all-to-all-start.1 = ((bf16[4,2,7168]{2,1,0:T(2,128)(2,1)}), bf16[4,2,7168]{2,1,0:T(2,128)(2,1)S(1)}, u32[]{:S(2)}, u32[]{:S(2)}) async-start(bf16[4,2,7168]{2,1,0:T(2,128)(2,1)} %copy.66), calls=%async_computation.1 | async-start | bytes 229376 | tf_op jit(solution)/shard_map/all_to_all | solution.py:131
  126.5 46.6 %all-reduce.6.cloned.1.call-start = ((), (), s32[]{:S(2)}) async-start(), calls=%async_computation.4 | async-start | bytes 131072 | tf_op jit(solution)/shard_map/psum | solution.py:107
  129.0 0.6 copy-start.13
  133.0 17.8 %all-to-all-start = ((bf16[4,2,7168]{2,1,0:T(2,128)(2,1)}), bf16[4,2,7168]{2,1,0:T(2,128)(2,1)S(1)}, u32[]{:S(2)}, u32[]{:S(2)}) async-start(bf16[4,2,7168]{2,1,0:T(2,128)(2,1)} %convolution_convert_fusion.1), calls=%async_computation | async-start | bytes 229376 | tf_op jit(solution)/shard_map/all_to_all | solution.py:132
  136.5 88.9 %all-reduce.8.cloned.1.call-start = ((), (), s32[]{:S(2)}) async-start(), calls=%async_computation.5 | async-start | bytes 1835008
  146.9 3.2 %copy-start.5 = (bf16[1,7168,256]{2,1,0:T(8,128)(2,1)S(1)}, bf16[1,7168,256]{2,1,0:T(8,128)(2,1)}, u32[]{:S(2)}) copy-start(bf16[1,7168,256]{2,1,0:T(8,128)(2,1)} %param.26) | copy-start | bytes 11010052
  161.0 3.5 %copy-start.7 = (bf16[1,7168,256]{2,1,0:T(8,128)(2,1)S(1)}, bf16[1,7168,256]{2,1,0:T(8,128)(2,1)}, u32[]{:S(2)}) copy-start(bf16[1,7168,256]{2,1,0:T(8,128)(2,1)} %param.25) | copy-start | bytes 11010052
  164.5 2.1 copy-start.6
  168.8 4.3 %copy-start.16 = (f32[128,8]{0,1:T(8,128)S(1)}, f32[128,8]{0,1:T(8,128)}, u32[]{:S(2)}) copy-start(f32[128,8]{0,1:T(8,128)} %param.22) | copy-start | bytes 12292
  173.1 67.3 %copy-start.12 = (bf16[64,512]{1,0:T(8,128)(2,1)S(1)}, bf16[64,512]{1,0:T(8,128)(2,1)}, u32[]{:S(2)}) copy-start(bf16[64,512]{1,0:T(8,128)(2,1)} %all-reduce.6.cloned.1.call-done) | copy-start | bytes 196612
  227.1 10.4 %all-to-all-start.2 = ((bf16[4,1,2,7168]{3,2,1,0:T(2,128)(2,1)}), bf16[4,1,2,7168]{3,2,1,0:T(2,128)(2,1)S(1)}, u32[]{:S(2)}, u32[]{:S(2)}) async-start(bf16[4,1,2,7168]{3,2,1,0:T(2,128)(2,1)} %copy.69), calls=%async_computation.2 | async-start | bytes 229376 | tf_op jit(solution)/shard_map/all_to_all | solution.py:160
Sparse Core Ops, SparseCore 0:
  130.2 35.4 all-reduce.5
  169.4 55.8 all-reduce.7
where the time goes:
time: 249 us; the launch traced here: 248 us
  matrix products  72.3 us (29%)
  blocking collectives  53.8 us (22%)
  waiting for transfers between devices  48.9 us (20%)
  local copies, waits for them, and re-layouts  32 us (13%)
  starting transfers between devices  19.9 us (8%)
  between operations  15.6 us (6%)
  other arithmetic  4.1 us (2%)
    unnamed x3, waiting for transfers between devices  28.3 us
    dot_general x8, matrix products, backward_terms(): jnp.einsum('hqk,kl->qhl', score_grad, key_block, preferred_element_type=j...  24.2 us
    unnamed x2, blocking collectives  22.9 us
    while x63, local copies, waits for them, and re-layouts  16.5 us
    dot_general x16, matrix products, masked_scores(): jnp.einsum('qhl,kl->hqk', queries, key_block, preferred_element_type=jnp....  14.4 us
    unnamed x40, local copies, waits for them, and re-layouts  12.4 us
    ppermute x22, waiting for transfers between devices, passed_along(): lax.ppermute(array, axis, [(i, (i + by) % count) for i in range(count)])  12.1 us
    all_gather x1, blocking collectives, expert_grads(): piece_in = lax.all_gather(recv_in, 'ctx', axis=0, tiled=True)  10.4 us
  transfers between devices with their start and end apart: 27, of which 14 were waited for; matrix products, arithmetic and copies ran while one was open for 27% of the time, Pallas kernels for 0%

commit v1 on v0

--- a/solution.py
+++ b/solution.py
@@ -133,8 +133,11 @@
     )
     recv_in = recv_in.reshape(exp_size, per_device, CAP, model_width)
     recv_grad = recv_grad.reshape(exp_size, per_device, CAP, model_width)
-    piece_in = lax.all_gather(recv_in, "ctx", axis=0, tiled=True)
-    piece_grad = lax.all_gather(recv_grad, "ctx", axis=0, tiled=True)
+    piece_in, piece_grad = jnp.split(
+        lax.all_gather(jnp.concatenate([recv_in, recv_grad], axis=1), "ctx", axis=0, tiled=True),
+        [recv_in.shape[1]],
+        axis=1,
+    )
     gate_pre = jnp.einsum("necd,edh->nech", piece_in, w_gate, preferred_element_type=jnp.float32)
     up_pre = jnp.einsum("necd,edh->nech", piece_in, w_up, preferred_element_type=jnp.float32)
     act_grad = jnp.einsum("necd,ehd->nech", piece_grad, w_down, preferred_element_type=jnp.float32)

time: 249 us -> 263 us (1.056)
  waiting for transfers between devices: 48.9 us -> 79.1 us
  blocking collectives: 53.8 us -> 28.9 us
  local copies, waits for them, and re-layouts: 32 us -> 37.3 us
  matrix products: 72.3 us -> 67.8 us
  other arithmetic: 4.1 us -> 6.99 us
  starting transfers between devices: 19.9 us -> 22.7 us
    all_gather x2 -> x0, blocking collectives: 20.7 us -> none  [the longest x1 10.4 us: expert_grads(): piece_in = lax.all_gather(recv_in, 'ctx', axis=0, tiled=True)]
    psum x1, waiting for transfers between devices: 0.02 us -> 15 us  [attention_grads(): d_latent = lax.psum(own_latent.astype(jnp.bfloat16), 'exp')]
    unnamed x3 -> x4, waiting for transfers between devices: 28.3 us -> 37.5 us
    ppermute x22, waiting for transfers between devices: 12.1 us -> 18.7 us  [passed_along(): lax.ppermute(array, axis, [(i, (i + by) % count) for i in range(count)])]
    all_to_all x1, waiting for transfers between devices: 3.3 us -> 0.01 us  [expert_grads(): lax.all_to_all(send_in, 'exp', split_axis=0, concat_axis=0, tiled=True)]
    unnamed x2, blocking collectives: 22.9 us -> 20 us
    split x0 -> x1, local copies, waits for them, and re-layouts: none -> 2.87 us  [expert_grads(): jnp.split(lax.all_gather(jnp.concatenate([recv_in, recv_grad], axis=1), '...]
    all_to_all x1, waiting for transfers between devices: 0.01 us -> 2.71 us  [expert_grads(): lax.all_to_all(send_grad, 'exp', split_axis=0, concat_axis=0, tiled=True)]
  transfers between devices with their start and end apart: 27 -> 28, of which waited for: 14 -> 18; matrix products, arithmetic and copies ran while one was open for 27% -> 31% of each run, Pallas kernels for 0% -> 0%
where the time goes in v1:
time: 263 us; the launch traced here: 261 us
  waiting for transfers between devices  79.1 us (30%)
  matrix products  67.8 us (26%)
  local copies, waits for them, and re-layouts  37.3 us (14%)
  blocking collectives  28.9 us (11%)
  starting transfers between devices  22.7 us (9%)
  between operations  17.1 us (7%)
  other arithmetic  6.99 us (3%)
    unnamed x4, waiting for transfers between devices  37.5 us
    dot_general x8, matrix products, backward_terms(): jnp.einsum('hqk,kl->qhl', score_grad, key_block, preferred_element_type=j...  24.2 us
    unnamed x2, blocking collectives  20 us
    ppermute x22, waiting for transfers between devices, passed_along(): lax.ppermute(array, axis, [(i, (i + by) % count) for i in range(count)])  18.7 us
    while x63, local copies, waits for them, and re-layouts  16.6 us
    psum x1, waiting for transfers between devices, attention_grads(): d_latent = lax.psum(own_latent.astype(jnp.bfloat16), 'exp')  15 us
    dot_general x16, matrix products, masked_scores(): jnp.einsum('qhl,kl->hqk', queries, key_block, preferred_element_type=jnp....  14.4 us
    unnamed x43, local copies, waits for them, and re-layouts  13.1 us
  transfers between devices with their start and end apart: 28, of which 18 were waited for; matrix products, arithmetic and copies ran while one was open for 31% of the time, Pallas kernels for 0%

profile of v1, /device:TPU:0, one launch (start us, length us, event | category | flops | bytes accessed | tf_op | source)
XLA Modules:
  0.0 261.2 jit_solution(4286277584514413014)
XLA Ops:
  8.0 1.0 copy.158
  9.7 0.9 fusion.75
  11.8 6.3 %all-to-all-start = ((bf16[4,2,7168]{2,1,0:T(2,128)(2,1)}), bf16[4,2,7168]{2,1,0:T(2,128)(2,1)S(1)}, u32[]{:S(2)}, u32[]{:S(2)}) async-start(bf16[4,2,7168]{2,1,0:T(2,128)(2,1)} %copy.65), calls=%async_computation | async-start | bytes 229376 | tf_op jit(solution)/shard_map/all_to_all | solution.py:131
  19.6 8.0 %all-reduce = s32[512]{0:T(512)S(1)} all-reduce(s32[512]{0:T(512)S(1)} %dynamic-update-slice), channel_id=1, replica_groups=mesh['ctx'=8,'exp'=4] {'ctx'}, use_global_device_ids=true, to_apply=%add | all-reduce | flops 512 | bytes 4096
  27.7 1.8 copy.58
  29.5 2.8 %copy.59 = bf16[64,16,512]{2,0,1:T(8,128)(2,1)} copy(bf16[64,16,512]{2,1,0:T(8,128)(2,1)} %param.18) | data formatting | bytes 2097152
  32.5 32.2 %while.42 = (s32[]{:T(128)}, bf16[64,512]{1,0:T(8,128)(2,1)S(1)}, f32[16,64]{1,0:T(8,128)S(1)}, f32[16,64]{1,0:T(8,128)S(1)}, f32[16,64,512]{2,1,0:T(8,128)}, /*...) while((s32[]{:T(128)}, bf16[64,512]{1,0:T(8,128)(2,1)S(1)}, ...), condition=%wide.region_3.4_spmd.clone, body=%wide.region_0.3_spmd.clone.sunk | while | flops 136258576 | bytes 23405988 | solution.py:66
  34.8 1.3 copy-done.3
  36.1 1.1 collective-permute-done
  39.3 1.3 copy-done.3
  40.7 1.1 collective-permute-done
  43.9 1.3 copy-done.3
  45.3 1.1 collective-permute-done
  48.5 1.3 copy-done.3
  49.9 1.1 collective-permute-done
  53.1 1.3 copy-done.3
  54.4 1.1 collective-permute-done
  57.7 1.3 copy-done.3
  59.0 1.1 collective-permute-done
  62.3 1.3 copy-done.3
  63.6 1.1 collective-permute-done
  64.7 2.7 %fusion.106 = (f32[16,64]{1,0:T(8,128)S(1)}, f32[16,64,64]{1,2,0:T(8,128)S(1)}) fusion(bf16[64,16,512]{2,1,0:T(8,128)(2,1)} %param.16, bf16[64,512]{1,0:T(8,128)(2,1)S(1)} %get-tuple-element.496, pred[64,64]{0,1:T(8,128)(4,1)S(1)} %get-tuple-element.694), kind=kOutput, calls=%fused_computation.142 | convolution fusion | flops 67304448 | bytes 1384448 | tf_op jit(solution)/shard_map/qhl,kl->hqk/dot_general | solution.py:35
  67.6 1.8 add_divide_fusion
  70.5 5.1 %all-to-all-start.1 = ((bf16[4,2,7168]{2,1,0:T(2,128)(2,1)}), bf16[4,2,7168]{2,1,0:T(2,128)(2,1)S(1)}, u32[]{:S(2)}, u32[]{:S(2)}) async-start(bf16[4,2,7168]{2,1,0:T(2,128)(2,1)} %copy.66), calls=%async_computation.1 | async-start | bytes 229376 | tf_op jit(solution)/shard_map/all_to_all | solution.py:132
  75.6 3.1 %multiply_reduce_fusion = f32[16,64]{0,1:T(8,128)S(1)} fusion(f32[16,64,512]{2,1,0:T(8,128)} %add_divide_fusion, bf16[64,16,512]{2,1,0:T(8,128)(2,1)} %param.18), kind=kLoop, calls=%fused_computation.55 | loop fusion | flops 1571840 | bytes 3149824
  78.8 2.7 %all-to-all-done.1 = bf16[4,2,7168]{2,1,0:T(2,128)(2,1)S(1)} async-done(((bf16[4,2,7168]{2,1,0:T(2,128)(2,1)}), bf16[4,2,7168]{2,1,0:T(2,128)(2,1)S(1)}, u32[]{:S(2)}, u32[]{:S(2)}) %all-to-all-start.1) | async-done | bytes 114720 | tf_op jit(solution)/shard_map/all_to_all | solution.py:132
  81.8 0.8 copy.67
  83.0 53.0 %while.43 = (s32[]{:T(128)}, bf16[64,512]{1,0:T(8,128)(2,1)S(1)}, f32[64,512]{1,0:T(8,128)S(1)}, f32[64,16,512]{2,0,1:T(8,128)}, s32[]{:T(128)}, /*index=5*/s32[...) while((s32[]{:T(128)}, bf16[64,512]{1,0:T(8,128)(2,1)S(1)}, ...), condition=%wide.region_7.8_spmd.clone, body=%wide.region_6.7_spmd.clone.sunk | while | flops 337776640 | bytes 15287743 | solution.py:101
  86.1 1.8 bitcast_add_fusion.3
  87.9 2.4 collective-permute-done.2
  93.0 3.4 %bitcast_add_fusion.3 = f32[64,16,512]{2,0,1:T(8,128)} fusion(f32[64,16,512]{2,0,1:T(8,128)} %get-tuple-element.894, bf16[16,64,64]{1,2,0:T(8,128)(2,1)S(1)} %fusion.158, pred[]{:T(512)S(6)} %compare.11, bf16[64,512]{1,0:T(8,128)(2,1)S(1)} %copy.147), kind=kOutput, calls=%fused_computation.16.clone.1 | convolution fusion | flops 68681728 | bytes 4390913 | tf_op jit(solution)/shard_map/while/body/eval_jaxpr/hqk,kl->qhl/dot_general | solution.py:81
  96.4 1.2 collective-permute-done.2
  100.3 1.0 collective-permute-start.2
  101.3 3.4 %bitcast_add_fusion.3 = f32[64,16,512]{2,0,1:T(8,128)} fusion(f32[64,16,512]{2,0,1:T(8,128)} %get-tuple-element.894, bf16[16,64,64]{1,2,0:T(8,128)(2,1)S(1)} %fusion.158, pred[]{:T(512)S(6)} %compare.11, bf16[64,512]{1,0:T(8,128)(2,1)S(1)} %copy.147), kind=kOutput, calls=%fused_computation.16.clone.1 | convolution fusion | flops 68681728 | bytes 4390913 | tf_op jit(solution)/shard_map/while/body/eval_jaxpr/hqk,kl->qhl/dot_general | solution.py:81
  104.7 1.6 collective-permute-done.2
  109.2 3.4 %bitcast_add_fusion.3 = f32[64,16,512]{2,0,1:T(8,128)} fusion(f32[64,16,512]{2,0,1:T(8,128)} %get-tuple-element.894, bf16[16,64,64]{1,2,0:T(8,128)(2,1)S(1)} %fusion.158, pred[]{:T(512)S(6)} %compare.11, bf16[64,512]{1,0:T(8,128)(2,1)S(1)} %copy.147), kind=kOutput, calls=%fused_computation.16.clone.1 | convolution fusion | flops 68681728 | bytes 4390913 | tf_op jit(solution)/shard_map/while/body/eval_jaxpr/hqk,kl->qhl/dot_general | solution.py:81
  112.6 1.0 collective-permute-done.2
  116.2 1.0 collective-permute-start.2
  117.3 3.4 %bitcast_add_fusion.3 = f32[64,16,512]{2,0,1:T(8,128)} fusion(f32[64,16,512]{2,0,1:T(8,128)} %get-tuple-element.894, bf16[16,64,64]{1,2,0:T(8,128)(2,1)S(1)} %fusion.158, pred[]{:T(512)S(6)} %compare.11, bf16[64,512]{1,0:T(8,128)(2,1)S(1)} %copy.147), kind=kOutput, calls=%fused_computation.16.clone.1 | convolution fusion | flops 68681728 | bytes 4390913 | tf_op jit(solution)/shard_map/while/body/eval_jaxpr/hqk,kl->qhl/dot_general | solution.py:81
  123.6 1.0 collective-permute-start.2
  124.6 3.4 %bitcast_add_fusion.3 = f32[64,16,512]{2,0,1:T(8,128)} fusion(f32[64,16,512]{2,0,1:T(8,128)} %get-tuple-element.894, bf16[16,64,64]{1,2,0:T(8,128)(2,1)S(1)} %fusion.158, pred[]{:T(512)S(6)} %compare.11, bf16[64,512]{1,0:T(8,128)(2,1)S(1)} %copy.147), kind=kOutput, calls=%fused_computation.16.clone.1 | convolution fusion | flops 68681728 | bytes 4390913 | tf_op jit(solution)/shard_map/while/body/eval_jaxpr/hqk,kl->qhl/dot_general | solution.py:81
  130.9 1.7 collective-permute-start.2
  132.6 3.4 %bitcast_add_fusion.3 = f32[64,16,512]{2,0,1:T(8,128)} fusion(f32[64,16,512]{2,0,1:T(8,128)} %get-tuple-element.894, bf16[16,64,64]{1,2,0:T(8,128)(2,1)S(1)} %fusion.158, pred[]{:T(512)S(6)} %compare.11, bf16[64,512]{1,0:T(8,128)(2,1)S(1)} %copy.147), kind=kOutput, calls=%fused_computation.16.clone.1 | convolution fusion | flops 68681728 | bytes 4390913 | tf_op jit(solution)/shard_map/while/body/eval_jaxpr/hqk,kl->qhl/dot_general | solution.py:81
  136.0 2.7 %fusion.45 = f32[16,64,64]{1,2,0:T(8,128)S(1)} fusion(f32[16,64]{1,0:T(8,128)S(1)} %get-tuple-element.952, pred[64,64]{0,1:T(8,128)(4,1)S(1)} %get-tuple-element.693, bf16[64,512]{1,0:T(8,128)(2,1)S(1)} %get-tuple-element.500, bf16[64,16,512]{2,1,0:T(8,128)(2,1)} %param.16), kind=kOutput, calls=%fused_computation.66 | convolution fusion | flops 67305472 | bytes 1384448 | tf_op jit(solution)/shard_map/qhl,kl->hqk/dot_general | solution.py:35
  138.7 1.2 convolution_bitcast_fusion.5
  140.0 1.3 fusion.48
  141.3 1.2 fusion.52
  142.7 4.5 %collective-permute-done.3 = bf16[64,512]{1,0:T(8,128)(2,1)S(1)} collective-permute-done((bf16[64,512]{1,0:T(8,128)(2,1)S(1)}, bf16[64,512]{1,0:T(8,128)(2,1)S(1)}, u32[]{:S(2)}, u32[]{:S(2)}) %collective-permute-start.3) | collective-permute-done | bytes 65568 | tf_op jit(solution)/shard_map/ppermute | solution.py:12
  148.2 2.9 %fusion.103 = (bf16[32,1,2,7168]{3,2,1,0:T(2,128)(2,1)S(1)}, bf16[32,1,2,7168]{3,2,1,0:T(2,128)(2,1)S(1)}) fusion(bf16[32,2,2,7168]{3,2,1,0:T(2,128)(2,1)} %all-gather.2.cloned.1.call-done), kind=kLoop, calls=%fused_computation.139 | loop fusion | bytes 3670016 | tf_op jit(solution)/shard_map/split | solution.py:136
  151.7 1.4 copy-done.5
  153.8 1.4 copy-done.11
  155.1 1.3 multiply_reduce_fusion.1
  156.4 1.2 fusion.28
  157.7 2.2 fusion.27
  159.9 2.1 fusion.37
  162.0 1.5 copy.74
  164.2 15.0 %all-reduce.6.cloned.1.call-done = bf16[64,512]{1,0:T(8,128)(2,1)} async-done(((bf16[64,512]{1,0:T(8,128)(2,1)}), bf16[64,512]{1,0:T(8,128)(2,1)}) %all-reduce.6.cloned.1.call-update) | async-done | bytes 65552 | tf_op jit(solution)/shard_map/psum | solution.py:107
  179.2 12.0 %all-reduce.2 = bf16[32,1,2]{0,2,1:T(2,128)(2,1)S(1)} all-reduce(f32[32,1,2]{0,2,1:T(2,128)S(1)} %bitcast.247), channel_id=3, replica_groups=mesh['ctx'=8,'exp'=4] {'ctx'}, use_global_device_ids=true, to_apply=%region_13.14.clone | all-reduce | flops 64 | bytes 384
  191.3 8.9 %all_to_all.20 = bf16[4,1,2]{2,1,0:T(2,128)(2,1)S(1)} all-to-all(bf16[4,1,2]{2,1,0:T(2,128)(2,1)S(1)} %copy.72), channel_id=1, replica_groups=mesh['ctx'=8,'exp'=4] {'exp'}, dimensions={0} | all-to-all | bytes 32 | tf_op jit(solution)/shard_map/all_to_all | solution.py:164
  200.4 37.5 %all-reduce.8.cloned.1.call-done = bf16[32,1,2,7168]{3,0,2,1:T(8,128)(2,1)} async-done(((bf16[32,1,2,7168]{3,0,2,1:T(8,128)(2,1)}), bf16[32,1,2,7168]{3,0,2,1:T(8,128)(2,1)}) %all-reduce.8.cloned.1.call-update) | async-done | bytes 917520
  237.9 1.0 constant_dynamic-slice_fusion
  239.7 4.6 %all-to-all-start.2 = ((bf16[4,1,2,7168]{3,2,1,0:T(2,128)(2,1)}), bf16[4,1,2,7168]{3,2,1,0:T(2,128)(2,1)S(1)}, u32[]{:S(2)}, u32[]{:S(2)}) async-start(bf16[4,1,2,7168]{3,2,1,0:T(2,128)(2,1)} %copy.70), calls=%async_computation.2 | async-start | bytes 229376 | tf_op jit(solution)/shard_map/all_to_all | solution.py:163
  245.0 5.2 %all-to-all-done.2 = bf16[4,1,2,7168]{3,2,1,0:T(2,128)(2,1)S(1)} async-done(((bf16[4,1,2,7168]{3,2,1,0:T(2,128)(2,1)}), bf16[4,1,2,7168]{3,2,1,0:T(2,128)(2,1)S(1)}, u32[]{:S(2)}, u32[]{:S(2)}) %all-to-all-start.2) | async-done | bytes 114720 | tf_op jit(solution)/shard_map/all_to_all | solution.py:163
  250.2 2.9 %fusion.25 = bf16[128,7168]{1,0:T(8,128)(2,1)} fusion(bf16[4,1,2,7168]{3,2,1,0:T(2,128)(2,1)S(1)} %all-to-all-done.2, pred[128,4,2]{0,1,2:T(4,128)(4,1)S(1)} %fusion.91, f32[128,4]{0,1:T(4,128)S(1)} %fusion.84), kind=kOutput, calls=%fused_computation.38 | convolution fusion | flops 88998912 | bytes 1952768 | tf_op jit(solution)/shard_map/tes,esd->td/dot_general | solution.py:172
  (255 shorter events, 43.9 us)
Async XLA Ops:
  8.0 2.7 %copy-start = (bf16[128,7168]{1,0:T(8,128)(2,1)S(1)}, bf16[128,7168]{1,0:T(8,128)(2,1)}, u32[]{:S(2)}) copy-start(bf16[128,7168]{1,0:T(8,128)(2,1)} %param.20) | copy-start | bytes 5505028
  8.0 10.1 %copy-start.19 = (u32[32]{0:T(128)S(1)}, u32[32]{0:T(128)}, u32[]{:S(2)}) copy-start(u32[32]{0:T(128)} %constant.232) | copy-start | bytes 388
  8.0 11.4 %copy-start.16 = (s32[64]{0:T(128)S(1)}, s32[64]{0:T(128)}, u32[]{:S(2)}) copy-start(s32[64]{0:T(128)} %param.19) | copy-start | bytes 772
  9.0 20.5 %copy-start.8 = (bf16[64,512]{1,0:T(8,128)(2,1)}, bf16[64,512]{1,0:T(8,128)(2,1)S(1)}, u32[]{:S(2)}) copy-start(bf16[64,512]{1,0:T(8,128)(2,1)S(1)} %copy.158) | copy-start | bytes 196612
  11.8 58.8 %all-to-all-start = ((bf16[4,2,7168]{2,1,0:T(2,128)(2,1)}), bf16[4,2,7168]{2,1,0:T(2,128)(2,1)S(1)}, u32[]{:S(2)}, u32[]{:S(2)}) async-start(bf16[4,2,7168]{2,1,0:T(2,128)(2,1)} %copy.65), calls=%async_computation | async-start | bytes 229376 | tf_op jit(solution)/shard_map/all_to_all | solution.py:131
  29.5 3.0 %copy-start.10 = (bf16[64,512]{1,0:T(8,128)(2,1)S(1)}, bf16[64,512]{1,0:T(8,128)(2,1)}, u32[]{:S(2)}) copy-start(bf16[64,512]{1,0:T(8,128)(2,1)} %copy-done.8) | copy-start | bytes 196612
  32.5 4.6 %collective-permute-start = (bf16[64,512]{1,0:T(8,128)(2,1)S(1)}, bf16[64,512]{1,0:T(8,128)(2,1)S(1)}, u32[]{:S(2)}, u32[]{:S(2)}) collective-permute-start(bf16[64,512]{1,0:T(8,128)(2,1)S(1)} %copy.133), channel_id=1, source_target_pairs={{0,4},{4,8},{8,12},{12,16},{16,20},{20,24},{24,28},{28,0},{1,5},{5... | collective-permute-start | bytes 196616 | tf_op jit(solution)/shard_map/while/body/eval_jaxpr/ppermute | solution.py:12
  32.6 1.6 copy-start.2
  34.7 1.3 copy-start.3
  37.1 4.6 %collective-permute-start = (bf16[64,512]{1,0:T(8,128)(2,1)S(1)}, bf16[64,512]{1,0:T(8,128)(2,1)S(1)}, u32[]{:S(2)}, u32[]{:S(2)}) collective-permute-start(bf16[64,512]{1,0:T(8,128)(2,1)S(1)} %copy.133), channel_id=1, source_target_pairs={{0,4},{4,8},{8,12},{12,16},{16,20},{20,24},{24,28},{28,0},{1,5},{5... | collective-permute-start | bytes 196616 | tf_op jit(solution)/shard_map/while/body/eval_jaxpr/ppermute | solution.py:12
  37.2 1.6 copy-start.2
  39.3 1.3 copy-start.3
  41.7 4.6 %collective-permute-start = (bf16[64,512]{1,0:T(8,128)(2,1)S(1)}, bf16[64,512]{1,0:T(8,128)(2,1)S(1)}, u32[]{:S(2)}, u32[]{:S(2)}) collective-permute-start(bf16[64,512]{1,0:T(8,128)(2,1)S(1)} %copy.133), channel_id=1, source_target_pairs={{0,4},{4,8},{8,12},{12,16},{16,20},{20,24},{24,28},{28,0},{1,5},{5... | collective-permute-start | bytes 196616 | tf_op jit(solution)/shard_map/while/body/eval_jaxpr/ppermute | solution.py:12
  41.8 1.6 copy-start.2
  43.9 1.3 copy-start.3
  46.3 4.6 %collective-permute-start = (bf16[64,512]{1,0:T(8,128)(2,1)S(1)}, bf16[64,512]{1,0:T(8,128)(2,1)S(1)}, u32[]{:S(2)}, u32[]{:S(2)}) collective-permute-start(bf16[64,512]{1,0:T(8,128)(2,1)S(1)} %copy.133), channel_id=1, source_target_pairs={{0,4},{4,8},{8,12},{12,16},{16,20},{20,24},{24,28},{28,0},{1,5},{5... | collective-permute-start | bytes 196616 | tf_op jit(solution)/shard_map/while/body/eval_jaxpr/ppermute | solution.py:12
  46.4 1.6 copy-start.2
  48.5 1.3 copy-start.3
  50.9 4.6 %collective-permute-start = (bf16[64,512]{1,0:T(8,128)(2,1)S(1)}, bf16[64,512]{1,0:T(8,128)(2,1)S(1)}, u32[]{:S(2)}, u32[]{:S(2)}) collective-permute-start(bf16[64,512]{1,0:T(8,128)(2,1)S(1)} %copy.133), channel_id=1, source_target_pairs={{0,4},{4,8},{8,12},{12,16},{16,20},{20,24},{24,28},{28,0},{1,5},{5... | collective-permute-start | bytes 196616 | tf_op jit(solution)/shard_map/while/body/eval_jaxpr/ppermute | solution.py:12
  51.0 1.6 copy-start.2
  53.1 1.3 copy-start.3
  55.5 4.6 %collective-permute-start = (bf16[64,512]{1,0:T(8,128)(2,1)S(1)}, bf16[64,512]{1,0:T(8,128)(2,1)S(1)}, u32[]{:S(2)}, u32[]{:S(2)}) collective-permute-start(bf16[64,512]{1,0:T(8,128)(2,1)S(1)} %copy.133), channel_id=1, source_target_pairs={{0,4},{4,8},{8,12},{12,16},{16,20},{20,24},{24,28},{28,0},{1,5},{5... | collective-permute-start | bytes 196616 | tf_op jit(solution)/shard_map/while/body/eval_jaxpr/ppermute | solution.py:12
  55.6 1.6 copy-start.2
  57.7 1.3 copy-start.3
  60.1 4.6 %collective-permute-start = (bf16[64,512]{1,0:T(8,128)(2,1)S(1)}, bf16[64,512]{1,0:T(8,128)(2,1)S(1)}, u32[]{:S(2)}, u32[]{:S(2)}) collective-permute-start(bf16[64,512]{1,0:T(8,128)(2,1)S(1)} %copy.133), channel_id=1, source_target_pairs={{0,4},{4,8},{8,12},{12,16},{16,20},{20,24},{24,28},{28,0},{1,5},{5... | collective-permute-start | bytes 196616 | tf_op jit(solution)/shard_map/while/body/eval_jaxpr/ppermute | solution.py:12
  60.2 1.6 copy-start.2
  62.3 1.3 copy-start.3
  64.7 2.9 %copy-start.4 = (f32[16,64,512]{2,1,0:T(8,128)S(1)}, f32[16,64,512]{2,1,0:T(8,128)}, u32[]{:S(2)}) copy-start(f32[16,64,512]{2,1,0:T(8,128)} %get-tuple-element.498) | copy-start | bytes 6291460
  67.6 1.8 copy-start.12
  70.5 11.0 %all-to-all-start.1 = ((bf16[4,2,7168]{2,1,0:T(2,128)(2,1)}), bf16[4,2,7168]{2,1,0:T(2,128)(2,1)S(1)}, u32[]{:S(2)}, u32[]{:S(2)}) async-start(bf16[4,2,7168]{2,1,0:T(2,128)(2,1)} %copy.66), calls=%async_computation.1 | async-start | bytes 229376 | tf_op jit(solution)/shard_map/all_to_all | solution.py:132
  75.6 7.3 %copy-start.9 = (bf16[64,512]{1,0:T(8,128)(2,1)S(1)}, bf16[64,512]{1,0:T(8,128)(2,1)}, u32[]{:S(2)}) copy-start(bf16[64,512]{1,0:T(8,128)(2,1)} %copy-done.8) | copy-start | bytes 196612
  75.6 72.5 %all-gather.2.cloned.1.call-start = ((), (), s32[]{:S(2)}) async-start(), calls=%async_computation.5 | async-start | bytes 2064384 | tf_op jit(solution)/shard_map/all_gather | solution.py:137
  82.7 96.4 %all-reduce.6.cloned.1.call-start = ((), (), s32[]{:S(2)}) async-start(), calls=%async_computation.4 | async-start | bytes 131072 | tf_op jit(solution)/shard_map/psum | solution.py:107
  83.0 7.3 %collective-permute-start.1 = (bf16[64,512]{1,0:T(8,128)(2,1)S(1)}, bf16[64,512]{1,0:T(8,128)(2,1)S(1)}, u32[]{:S(2)}, u32[]{:S(2)}) collective-permute-start(bf16[64,512]{1,0:T(8,128)(2,1)S(1)} %copy.147), channel_id=1, source_target_pairs={{0,4},{4,8},{8,12},{12,16},{16,20},{20,24},{24,28},{28,0},{1,5},{5... | collective-permute-start | bytes 196616 | tf_op jit(solution)/shard_map/while/body/eval_jaxpr/ppermute | solution.py:12
  83.1 1.2 copy-start.1
  85.6 4.6 %collective-permute-start.2 = (bf16[64,512]{1,0:T(8,128)(2,1)S(1)}, bf16[64,512]{1,0:T(8,128)(2,1)S(1)}, u32[]{:S(2)}, u32[]{:S(2)}) collective-permute-start(bf16[64,512]{1,0:T(8,128)(2,1)S(1)} %fusion.159), channel_id=1, source_target_pairs={{0,4},{4,8},{8,12},{12,16},{16,20},{20,24},{24,28},{28,0},{1,5},{5... | collective-permute-start | bytes 196616 | tf_op jit(solution)/shard_map/while/body/eval_jaxpr/ppermute | solution.py:12
  90.3 7.3 %collective-permute-start.1 = (bf16[64,512]{1,0:T(8,128)(2,1)S(1)}, bf16[64,512]{1,0:T(8,128)(2,1)S(1)}, u32[]{:S(2)}, u32[]{:S(2)}) collective-permute-start(bf16[64,512]{1,0:T(8,128)(2,1)S(1)} %copy.147), channel_id=1, source_target_pairs={{0,4},{4,8},{8,12},{12,16},{16,20},{20,24},{24,28},{28,0},{1,5},{5... | collective-permute-start | bytes 196616 | tf_op jit(solution)/shard_map/while/body/eval_jaxpr/ppermute | solution.py:12
  90.4 1.2 copy-start.1
  92.9 4.6 %collective-permute-start.2 = (bf16[64,512]{1,0:T(8,128)(2,1)S(1)}, bf16[64,512]{1,0:T(8,128)(2,1)S(1)}, u32[]{:S(2)}, u32[]{:S(2)}) collective-permute-start(bf16[64,512]{1,0:T(8,128)(2,1)S(1)} %fusion.159), channel_id=1, source_target_pairs={{0,4},{4,8},{8,12},{12,16},{16,20},{20,24},{24,28},{28,0},{1,5},{5... | collective-permute-start | bytes 196616 | tf_op jit(solution)/shard_map/while/body/eval_jaxpr/ppermute | solution.py:12
  97.6 8.6 %collective-permute-start.1 = (bf16[64,512]{1,0:T(8,128)(2,1)S(1)}, bf16[64,512]{1,0:T(8,128)(2,1)S(1)}, u32[]{:S(2)}, u32[]{:S(2)}) collective-permute-start(bf16[64,512]{1,0:T(8,128)(2,1)S(1)} %copy.147), channel_id=1, source_target_pairs={{0,4},{4,8},{8,12},{12,16},{16,20},{20,24},{24,28},{28,0},{1,5},{5... | collective-permute-start | bytes 196616 | tf_op jit(solution)/shard_map/while/body/eval_jaxpr/ppermute | solution.py:12
  97.7 1.2 copy-start.1
  100.3 5.9 %collective-permute-start.2 = (bf16[64,512]{1,0:T(8,128)(2,1)S(1)}, bf16[64,512]{1,0:T(8,128)(2,1)S(1)}, u32[]{:S(2)}, u32[]{:S(2)}) collective-permute-start(bf16[64,512]{1,0:T(8,128)(2,1)S(1)} %fusion.159), channel_id=1, source_target_pairs={{0,4},{4,8},{8,12},{12,16},{16,20},{20,24},{24,28},{28,0},{1,5},{5... | collective-permute-start | bytes 196616 | tf_op jit(solution)/shard_map/while/body/eval_jaxpr/ppermute | solution.py:12
  106.3 7.3 %collective-permute-start.1 = (bf16[64,512]{1,0:T(8,128)(2,1)S(1)}, bf16[64,512]{1,0:T(8,128)(2,1)S(1)}, u32[]{:S(2)}, u32[]{:S(2)}) collective-permute-start(bf16[64,512]{1,0:T(8,128)(2,1)S(1)} %copy.147), channel_id=1, source_target_pairs={{0,4},{4,8},{8,12},{12,16},{16,20},{20,24},{24,28},{28,0},{1,5},{5... | collective-permute-start | bytes 196616 | tf_op jit(solution)/shard_map/while/body/eval_jaxpr/ppermute | solution.py:12
  106.3 1.2 copy-start.1
  108.9 4.6 %collective-permute-start.2 = (bf16[64,512]{1,0:T(8,128)(2,1)S(1)}, bf16[64,512]{1,0:T(8,128)(2,1)S(1)}, u32[]{:S(2)}, u32[]{:S(2)}) collective-permute-start(bf16[64,512]{1,0:T(8,128)(2,1)S(1)} %fusion.159), channel_id=1, source_target_pairs={{0,4},{4,8},{8,12},{12,16},{16,20},{20,24},{24,28},{28,0},{1,5},{5... | collective-permute-start | bytes 196616 | tf_op jit(solution)/shard_map/while/body/eval_jaxpr/ppermute | solution.py:12
  113.6 7.3 %collective-permute-start.1 = (bf16[64,512]{1,0:T(8,128)(2,1)S(1)}, bf16[64,512]{1,0:T(8,128)(2,1)S(1)}, u32[]{:S(2)}, u32[]{:S(2)}) collective-permute-start(bf16[64,512]{1,0:T(8,128)(2,1)S(1)} %copy.147), channel_id=1, source_target_pairs={{0,4},{4,8},{8,12},{12,16},{16,20},{20,24},{24,28},{28,0},{1,5},{5... | collective-permute-start | bytes 196616 | tf_op jit(solution)/shard_map/while/body/eval_jaxpr/ppermute | solution.py:12
  116.2 4.6 %collective-permute-start.2 = (bf16[64,512]{1,0:T(8,128)(2,1)S(1)}, bf16[64,512]{1,0:T(8,128)(2,1)S(1)}, u32[]{:S(2)}, u32[]{:S(2)}) collective-permute-start(bf16[64,512]{1,0:T(8,128)(2,1)S(1)} %fusion.159), channel_id=1, source_target_pairs={{0,4},{4,8},{8,12},{12,16},{16,20},{20,24},{24,28},{28,0},{1,5},{5... | collective-permute-start | bytes 196616 | tf_op jit(solution)/shard_map/while/body/eval_jaxpr/ppermute | solution.py:12
  120.9 7.3 %collective-permute-start.1 = (bf16[64,512]{1,0:T(8,128)(2,1)S(1)}, bf16[64,512]{1,0:T(8,128)(2,1)S(1)}, u32[]{:S(2)}, u32[]{:S(2)}) collective-permute-start(bf16[64,512]{1,0:T(8,128)(2,1)S(1)} %copy.147), channel_id=1, source_target_pairs={{0,4},{4,8},{8,12},{12,16},{16,20},{20,24},{24,28},{28,0},{1,5},{5... | collective-permute-start | bytes 196616 | tf_op jit(solution)/shard_map/while/body/eval_jaxpr/ppermute | solution.py:12
  121.0 1.2 copy-start.1
  123.6 4.6 %collective-permute-start.2 = (bf16[64,512]{1,0:T(8,128)(2,1)S(1)}, bf16[64,512]{1,0:T(8,128)(2,1)S(1)}, u32[]{:S(2)}, u32[]{:S(2)}) collective-permute-start(bf16[64,512]{1,0:T(8,128)(2,1)S(1)} %fusion.159), channel_id=1, source_target_pairs={{0,4},{4,8},{8,12},{12,16},{16,20},{20,24},{24,28},{28,0},{1,5},{5... | collective-permute-start | bytes 196616 | tf_op jit(solution)/shard_map/while/body/eval_jaxpr/ppermute | solution.py:12
  128.2 7.7 %collective-permute-start.1 = (bf16[64,512]{1,0:T(8,128)(2,1)S(1)}, bf16[64,512]{1,0:T(8,128)(2,1)S(1)}, u32[]{:S(2)}, u32[]{:S(2)}) collective-permute-start(bf16[64,512]{1,0:T(8,128)(2,1)S(1)} %copy.147), channel_id=1, source_target_pairs={{0,4},{4,8},{8,12},{12,16},{16,20},{20,24},{24,28},{28,0},{1,5},{5... | collective-permute-start | bytes 196616 | tf_op jit(solution)/shard_map/while/body/eval_jaxpr/ppermute | solution.py:12
  128.3 1.2 copy-start.1
  130.9 5.1 %collective-permute-start.2 = (bf16[64,512]{1,0:T(8,128)(2,1)S(1)}, bf16[64,512]{1,0:T(8,128)(2,1)S(1)}, u32[]{:S(2)}, u32[]{:S(2)}) collective-permute-start(bf16[64,512]{1,0:T(8,128)(2,1)S(1)} %fusion.159), channel_id=1, source_target_pairs={{0,4},{4,8},{8,12},{12,16},{16,20},{20,24},{24,28},{28,0},{1,5},{5... | collective-permute-start | bytes 196616 | tf_op jit(solution)/shard_map/while/body/eval_jaxpr/ppermute | solution.py:12
  136.0 2.7 %copy-start.7 = (bf16[64,16,512]{2,1,0:T(8,128)(2,1)S(1)}, bf16[64,16,512]{2,1,0:T(8,128)(2,1)}, u32[]{:S(2)}) copy-start(bf16[64,16,512]{2,1,0:T(8,128)(2,1)} %param.18) | copy-start | bytes 3145732
  138.7 2.6 copy-start.13
  142.6 4.6 %collective-permute-start.3 = (bf16[64,512]{1,0:T(8,128)(2,1)S(1)}, bf16[64,512]{1,0:T(8,128)(2,1)S(1)}, u32[]{:S(2)}, u32[]{:S(2)}) collective-permute-start(bf16[64,512]{1,0:T(8,128)(2,1)S(1)} %fusion.52), channel_id=1, source_target_pairs={{0,4},{4,8},{8,12},{12,16},{16,20},{20,24},{24,28},{28,0},{1,5},{5... | collective-permute-start | bytes 196616 | tf_op jit(solution)/shard_map/ppermute | solution.py:12
  147.9 90.1 %all-reduce.8.cloned.1.call-start = ((), (), s32[]{:S(2)}) async-start(), calls=%async_computation.6 | async-start | bytes 1835008
  148.2 2.9 %copy-start.6 = (bf16[1,7168,256]{2,1,0:T(8,128)(2,1)S(1)}, bf16[1,7168,256]{2,1,0:T(8,128)(2,1)}, u32[]{:S(2)}) copy-start(bf16[1,7168,256]{2,1,0:T(8,128)(2,1)} %param.25) | copy-start | bytes 11010052
  151.1 2.0 copy-start.5
  153.1 2.0 copy-start.11
  159.9 4.3 %copy-start.17 = (s32[128,8]{0,1:T(8,128)S(1)}, s32[128,8]{0,1:T(8,128)}, u32[]{:S(2)}) copy-start(s32[128,8]{0,1:T(8,128)} %param.23) | copy-start | bytes 12292
  159.9 4.3 %copy-start.18 = (f32[128,8]{0,1:T(8,128)S(1)}, f32[128,8]{0,1:T(8,128)}, u32[]{:S(2)}) copy-start(f32[128,8]{0,1:T(8,128)} %param.22) | copy-start | bytes 12292
  179.2 74.0 %copy-start.14 = (bf16[64,512]{1,0:T(8,128)(2,1)S(1)}, bf16[64,512]{1,0:T(8,128)(2,1)}, u32[]{:S(2)}) copy-start(bf16[64,512]{1,0:T(8,128)(2,1)} %all-reduce.6.cloned.1.call-done) | copy-start | bytes 196612
  239.7 10.5 %all-to-all-start.2 = ((bf16[4,1,2,7168]{3,2,1,0:T(2,128)(2,1)}), bf16[4,1,2,7168]{3,2,1,0:T(2,128)(2,1)S(1)}, u32[]{:S(2)}, u32[]{:S(2)}) async-start(bf16[4,1,2,7168]{3,2,1,0:T(2,128)(2,1)} %copy.70), calls=%async_computation.2 | async-start | bytes 229376 | tf_op jit(solution)/shard_map/all_to_all | solution.py:163
  (2 other events, 1.9 us)
Sparse Core Ops, SparseCore 0:
  82.8 26.5 all-gather.1
Sparse Core Ops, SparseCore 1:
  147.9 31.1 all-reduce.5
  182.8 55.1 all-reduce.7
